TPU v7x, 32 devices: a whole 2x2x4 slice. The times are simulated.
32 devices in a mesh: slab: 8 (over z, y), band: 4 (over x, core).
Axes of the slice: x: 2, y: 2, z: 4, core: 2. Of those that a mesh axis runs over, the one named last changes fastest.
Arguments:
- orbitals: float32 [8, 128, 128, 128], P('band', 'slab'), may hold values from -6 to 6
Outputs:
- exchange_out: float32 [8, 128, 128, 128], P('band', 'slab')
All inputs are finite; a program needn't handle non-finite values.
Results may differ from a plain program's by a relative error of at most 0.00013.
Values sent between devices are 32-bit elements; how exact they have to be, the bound alone decides.
No kernel may reach another device: no remote copies, remote signals or barrier semaphores. Data moves between devices by JAX's collectives and lax.ppermute only.
A program may use at most 64 MiB of HBM per device.

v0:
```python
import math
import jax
import jax.numpy as jnp
from jax import lax
from jax.sharding import PartitionSpec as P

screen_width = 0.5
highest = lax.Precision.HIGHEST


def shifted(value, axis, steps):
    count = lax.axis_size(axis)
    pairs = [(source, (source + steps) % count) for source in range(count)]
    return lax.ppermute(value, axis, pairs)


def dft_tables(length):
    counter = jnp.arange(length, dtype=jnp.int32)
    product = counter[:, None] * counter[None, :] % length
    angles = 2.0 * math.pi / length * product.astype(jnp.float32)
    return (jnp.cos(angles), jnp.sin(angles))


def frequency(counter, length):
    return jnp.where(counter < length // 2, counter, counter - length).astype(jnp.float32)


def screened(squared):
    safe_sq = jnp.where(squared > 0, squared, 1.0)
    value = 4.0 * math.pi / safe_sq * (1.0 - jnp.exp(-safe_sq / (4.0 * screen_width**2)))
    return jnp.where(squared > 0, value, math.pi / screen_width**2)


def rotate(real_part, imag_part, cosine, sine_table, form, forward):
    sign = 1.0 if forward else -1.0
    real_cos = jnp.einsum(form, real_part, cosine, precision=highest)
    imag_sin = jnp.einsum(form, imag_part, sine_table, precision=highest)
    imag_cos = jnp.einsum(form, imag_part, cosine, precision=highest)
    real_sin = jnp.einsum(form, real_part, sine_table, precision=highest)
    return (real_cos + sign * imag_sin, imag_cos - sign * real_sin)


def potentials(density):
    count, planes, rows, columns = density.shape
    depth = planes * lax.axis_size("slab")
    cos_x, sin_x = dft_tables(columns)
    cos_y, sin_y = dft_tables(rows)
    cos_z, sin_z = dft_tables(depth)
    form_x = "pzyx,xk->pzyk"
    first = density[0::2]
    second = density[1::2]
    real_part = jnp.einsum(form_x, first, cos_x, precision=highest) + jnp.einsum(
        form_x, second, sin_x, precision=highest
    )
    imag_part = jnp.einsum(form_x, second, cos_x, precision=highest) - jnp.einsum(
        form_x, first, sin_x, precision=highest
    )
    real_part, imag_part = rotate(real_part, imag_part, cos_y, sin_y, "pzyx,yk->pzkx", True)
    part_re = lax.all_to_all(real_part, "slab", split_axis=2, concat_axis=1, tiled=True)
    part_im = lax.all_to_all(imag_part, "slab", split_axis=2, concat_axis=1, tiled=True)
    band_rows = part_re.shape[2]
    row_index = lax.axis_index("slab") * band_rows + jnp.arange(band_rows, dtype=jnp.int32)
    freq_z = frequency(jnp.arange(depth, dtype=jnp.int32), depth)
    freq_y = frequency(row_index, rows)
    freq_x = frequency(jnp.arange(columns, dtype=jnp.int32), columns)
    squared = ((2.0 * math.pi / depth * freq_z) ** 2)[:, None, None]
    squared = squared + ((2.0 * math.pi / rows * freq_y) ** 2)[None, :, None]
    squared = squared + ((2.0 * math.pi / columns * freq_x) ** 2)[None, None, :]
    weight = screened(squared)
    part_re, part_im = rotate(part_re, part_im, cos_z, sin_z, "pzyx,zk->pkyx", True)
    part_re = part_re * weight
    part_im = part_im * weight
    part_re, part_im = rotate(part_re, part_im, cos_z, sin_z, "pzyx,zk->pkyx", False)
    real_part = lax.all_to_all(part_re, "slab", split_axis=1, concat_axis=2, tiled=True)
    imag_part = lax.all_to_all(part_im, "slab", split_axis=1, concat_axis=2, tiled=True)
    real_part, imag_part = rotate(real_part, imag_part, cos_y, sin_y, "pzyx,yk->pzkx", False)
    factor = 1.0 / (columns * rows * depth)
    real_out = jnp.einsum(form_x, real_part, cos_x, precision=highest) - jnp.einsum(
        form_x, imag_part, sin_x, precision=highest
    )
    imag_out = jnp.einsum(form_x, imag_part, cos_x, precision=highest) + jnp.einsum(
        form_x, real_part, sin_x, precision=highest
    )
    stacked = jnp.stack([real_out * factor, imag_out * factor], axis=1)
    return stacked.reshape(count, planes, rows, columns)


def body(orbitals):
    count = orbitals.shape[0]
    grid_shape = orbitals.shape[1:]
    neighbour = shifted(orbitals, "band", 1)
    result = jnp.zeros_like(orbitals)
    for partners in (orbitals, neighbour):
        density = (orbitals[:, None] * partners[None, :]).reshape((count * count,) + grid_shape)
        field = potentials(density).reshape((count, count) + grid_shape)
        result = result - jnp.sum(field * partners[None], axis=1)
    return result


def solution(mesh):
    placed = (P("band", "slab", None, None),)
    return jax.shard_map(
        body, mesh=mesh, in_specs=placed, out_specs=P("band", "slab", None, None), check_vma=False
    )
```

profile of v0, /device:TPU:0, one launch (start us, length us, event | category | flops | bytes accessed | tf_op | source)
XLA Modules:
  0.0 544.5 jit_solution(10167117366901064484)
XLA Ops:
  0.0 2.7 broadcast_multiply_fusion.1
  18.6 7.3 %all-to-all-start.1 = ((f32[2,16,128,128]{3,1,0,2:T(8,128)}), f32[2,16,128,128]{3,1,0,2:T(8,128)}, u32[]{:S(2)}, u32[]{:S(2)}) async-start(f32[2,16,128,128]{3,1,0,2:T(8,128)} %copy.93), calls=%async_computation.1 | async-start | bytes 4194304 | tf_op jit(solution)/shard_map/all_to_all | solution.py:60
  25.9 3.7 fusion.140
  34.4 39.9 %all-to-all-done.1 = f32[2,16,128,128]{3,1,0,2:T(8,128)} async-done(((f32[2,16,128,128]{3,1,0,2:T(8,128)}), f32[2,16,128,128]{3,1,0,2:T(8,128)}, u32[]{:S(2)}, u32[]{:S(2)}) %all-to-all-start.1) | async-done | bytes 2097184 | tf_op jit(solution)/shard_map/all_to_all | solution.py:60
  74.3 4.6 all-to-all-start
  81.2 45.2 %all-to-all-done = f32[2,16,128,128]{3,1,0,2:T(8,128)} async-done(((f32[2,16,128,128]{3,1,0,2:T(8,128)}), f32[2,16,128,128]{3,1,0,2:T(8,128)}, u32[]{:S(2)}, u32[]{:S(2)}) %all-to-all-start) | async-done | bytes 2097184 | tf_op jit(solution)/shard_map/all_to_all | solution.py:59
  132.7 4.0 add_multiply_fusion.1
  141.4 2.7 add_bitcast_fusion.2
  146.7 4.3 all-to-all-start.2
  151.0 3.7 fusion.26
  159.6 39.2 %all-to-all-done.2 = f32[2,128,16,128]{3,2,0,1:T(8,128)} async-done(((f32[2,128,16,128]{3,2,0,1:T(8,128)}), f32[2,128,16,128]{3,2,0,1:T(8,128)}, u32[]{:S(2)}, u32[]{:S(2)}) %all-to-all-start.2) | async-done | bytes 2097184 | tf_op jit(solution)/shard_map/all_to_all | solution.py:74
  198.8 4.4 all-to-all-start.3
  203.5 3.2 copy.101
  206.7 44.3 %all-to-all-done.3 = f32[2,128,16,128]{3,2,0,1:T(8,128)} async-done(((f32[2,128,16,128]{3,2,0,1:T(8,128)}), f32[2,128,16,128]{3,2,0,1:T(8,128)}, u32[]{:S(2)}, u32[]{:S(2)}) %all-to-all-start.3) | async-done | bytes 2097184 | tf_op jit(solution)/shard_map/all_to_all | solution.py:75
  264.1 2.6 multiply_bitcast_fusion.3
  271.0 4.3 fusion
  288.6 2.6 copy.118
  291.2 4.3 all-to-all-start.5
  295.6 3.7 fusion.118
  304.1 39.3 %all-to-all-done.5 = f32[2,16,128,128]{3,1,0,2:T(8,128)} async-done(((f32[2,16,128,128]{3,1,0,2:T(8,128)}), f32[2,16,128,128]{3,1,0,2:T(8,128)}, u32[]{:S(2)}, u32[]{:S(2)}) %all-to-all-start.5) | async-done | bytes 2097184 | tf_op jit(solution)/shard_map/all_to_all | solution.py:60
  343.4 4.6 all-to-all-start.4
  349.8 45.7 %all-to-all-done.4 = f32[2,16,128,128]{3,1,0,2:T(8,128)} async-done(((f32[2,16,128,128]{3,1,0,2:T(8,128)}), f32[2,16,128,128]{3,1,0,2:T(8,128)}, u32[]{:S(2)}, u32[]{:S(2)}) %all-to-all-start.4) | async-done | bytes 2097184 | tf_op jit(solution)/shard_map/all_to_all | solution.py:59
  401.8 4.0 add_multiply_fusion
  410.5 2.7 add_bitcast_fusion
  413.2 2.6 copy.125
  415.8 4.3 all-to-all-start.6
  420.2 3.7 fusion.10
  428.8 39.2 %all-to-all-done.6 = f32[2,128,16,128]{3,2,0,1:T(8,128)} async-done(((f32[2,128,16,128]{3,2,0,1:T(8,128)}), f32[2,128,16,128]{3,2,0,1:T(8,128)}, u32[]{:S(2)}, u32[]{:S(2)}) %all-to-all-start.6) | async-done | bytes 2097184 | tf_op jit(solution)/shard_map/all_to_all | solution.py:74
  468.0 4.5 all-to-all-start.7
  474.4 45.8 %all-to-all-done.7 = f32[2,128,16,128]{3,2,0,1:T(8,128)} async-done(((f32[2,128,16,128]{3,2,0,1:T(8,128)}), f32[2,128,16,128]{3,2,0,1:T(8,128)}, u32[]{:S(2)}, u32[]{:S(2)}) %all-to-all-start.7) | async-done | bytes 2097184 | tf_op jit(solution)/shard_map/all_to_all | solution.py:75
  533.0 2.6 multiply_add_fusion
  539.8 2.8 fusion.1
  (78 shorter events, 114.9 us)
Async XLA Ops:
  13.6 2.4 copy-start.1
  18.6 55.7 %all-to-all-start.1 = ((f32[2,16,128,128]{3,1,0,2:T(8,128)}), f32[2,16,128,128]{3,1,0,2:T(8,128)}, u32[]{:S(2)}, u32[]{:S(2)}) async-start(f32[2,16,128,128]{3,1,0,2:T(8,128)} %copy.93), calls=%async_computation.1 | async-start | bytes 4194304 | tf_op jit(solution)/shard_map/all_to_all | solution.py:60
  74.3 52.2 %all-to-all-start = ((f32[2,16,128,128]{3,1,0,2:T(8,128)}), f32[2,16,128,128]{3,1,0,2:T(8,128)}, u32[]{:S(2)}, u32[]{:S(2)}) async-start(f32[2,16,128,128]{3,1,0,2:T(8,128)} %copy.88), calls=%async_computation | async-start | bytes 4194304 | tf_op jit(solution)/shard_map/all_to_all | solution.py:59
  81.2 49.3 %copy-start.5 = (f32[2,16,8,16,128]{4,1,2,3,0:T(8,128)}, f32[2,16,8,16,128]{4,1,2,3,0:T(8,128)S(1)}, u32[]{:S(2)}) copy-start(f32[2,16,8,16,128]{4,1,2,3,0:T(8,128)S(1)} %copy.94) | copy-start | bytes 6291460
  139.2 2.2 copy-start.4
  146.7 52.2 %all-to-all-start.2 = ((f32[2,128,16,128]{3,2,0,1:T(8,128)}), f32[2,128,16,128]{3,2,0,1:T(8,128)}, u32[]{:S(2)}, u32[]{:S(2)}) async-start(f32[2,128,16,128]{3,2,0,1:T(8,128)} %copy.100), calls=%async_computation.2 | async-start | bytes 4194304 | tf_op jit(solution)/shard_map/all_to_all | solution.py:74
  159.6 43.6 %copy-start = (f32[2,16,128,128]{3,2,1,0:T(8,128)S(1)}, f32[2,16,128,128]{3,2,1,0:T(8,128)}, u32[]{:S(2)}) copy-start(f32[2,16,128,128]{3,2,1,0:T(8,128)} %param.1) | copy-start | bytes 6291460
  198.8 52.2 %all-to-all-start.3 = ((f32[2,128,16,128]{3,2,0,1:T(8,128)}), f32[2,128,16,128]{3,2,0,1:T(8,128)}, u32[]{:S(2)}, u32[]{:S(2)}) async-start(f32[2,128,16,128]{3,2,0,1:T(8,128)} %copy.105), calls=%async_computation.3 | async-start | bytes 4194304 | tf_op jit(solution)/shard_map/all_to_all | solution.py:75
  203.2 67.8 %collective-permute-start = (f32[2,16,128,128]{3,2,1,0:T(8,128)S(1)}, f32[2,16,128,128]{3,2,1,0:T(8,128)}, u32[]{:S(2)}, u32[]{:S(2)}) collective-permute-start(f32[2,16,128,128]{3,2,1,0:T(8,128)S(1)} %copy-done), channel_id=1, source_target_pairs={{0,1},{1,2},{2,3},{3,0},{4,5},{5,6},{6,7},{7,4},{8,9},{9,10},{10,1... | collective-permute-start | bytes 6291464 | tf_op jit(solution)/shard_map/ppermute | solution.py:14
  252.8 2.2 copy-start.6
  286.4 2.2 copy-start.2
  291.2 52.2 %all-to-all-start.5 = ((f32[2,16,128,128]{3,1,0,2:T(8,128)}), f32[2,16,128,128]{3,1,0,2:T(8,128)}, u32[]{:S(2)}, u32[]{:S(2)}) async-start(f32[2,16,128,128]{3,1,0,2:T(8,128)} %copy.118), calls=%async_computation.5 | async-start | bytes 4194304 | tf_op jit(solution)/shard_map/all_to_all | solution.py:60
  343.4 52.2 %all-to-all-start.4 = ((f32[2,16,128,128]{3,1,0,2:T(8,128)}), f32[2,16,128,128]{3,1,0,2:T(8,128)}, u32[]{:S(2)}, u32[]{:S(2)}) async-start(f32[2,16,128,128]{3,1,0,2:T(8,128)} %copy.113), calls=%async_computation.4 | async-start | bytes 4194304 | tf_op jit(solution)/shard_map/all_to_all | solution.py:59
  349.8 49.8 %copy-start.7 = (f32[2,16,8,16,128]{4,1,2,3,0:T(8,128)}, f32[2,16,8,16,128]{4,1,2,3,0:T(8,128)S(1)}, u32[]{:S(2)}) copy-start(f32[2,16,8,16,128]{4,1,2,3,0:T(8,128)S(1)} %copy.119) | copy-start | bytes 6291460
  408.3 2.2 copy-start.3
  415.8 52.2 %all-to-all-start.6 = ((f32[2,128,16,128]{3,2,0,1:T(8,128)}), f32[2,128,16,128]{3,2,0,1:T(8,128)}, u32[]{:S(2)}, u32[]{:S(2)}) async-start(f32[2,128,16,128]{3,2,0,1:T(8,128)} %copy.125), calls=%async_computation.6 | async-start | bytes 4194304 | tf_op jit(solution)/shard_map/all_to_all | solution.py:74
  468.0 52.2 %all-to-all-start.7 = ((f32[2,128,16,128]{3,2,0,1:T(8,128)}), f32[2,128,16,128]{3,2,0,1:T(8,128)}, u32[]{:S(2)}, u32[]{:S(2)}) async-start(f32[2,128,16,128]{3,2,0,1:T(8,128)} %copy.130), calls=%async_computation.7 | async-start | bytes 4194304 | tf_op jit(solution)/shard_map/all_to_all | solution.py:75
  539.8 2.8 copy-start.8
where the time goes:
time: 554 us; the launch traced here: 544 us
  waiting for transfers between devices  338 us (61%)
  matrix products  117 us (21%)
  starting transfers between devices  38.6 us (7%)
  local copies, waits for them, and re-layouts  37.2 us (7%)
  other arithmetic  11.9 us (2%)
    all_to_all x2, waiting for transfers between devices, potentials(): lax.all_to_all(real_part, 'slab', split_axis=2, concat_axis=1, tiled=True)  90.9 us
    all_to_all x2, waiting for transfers between devices, potentials(): lax.all_to_all(part_im, 'slab', split_axis=1, concat_axis=2, tiled=True)  90.1 us
    all_to_all x2, waiting for transfers between devices, potentials(): lax.all_to_all(imag_part, 'slab', split_axis=2, concat_axis=1, tiled=True)  79.2 us
    all_to_all x2, waiting for transfers between devices, potentials(): lax.all_to_all(part_re, 'slab', split_axis=1, concat_axis=2, tiled=True)  78.3 us
    dot_general x8, matrix products, rotate(): real_cos = jnp.einsum(form, real_part, cosine, precision=highest)  21.7 us
    dot_general x8, matrix products, rotate(): imag_sin = jnp.einsum(form, imag_part, sine_table, precision=highest)  21.6 us
    dot_general x8, matrix products, rotate(): imag_cos = jnp.einsum(form, imag_part, cosine, precision=highest)  20.5 us
    dot_general x8, matrix products, rotate(): real_sin = jnp.einsum(form, real_part, sine_table, precision=highest)  18.9 us
  transfers between devices with their start and end apart: 9, of which 8 were waited for; matrix products, arithmetic and copies ran while one was open for 12% of the time, Pallas kernels for 0%

commit v1 on v0

--- a/solution.py
+++ b/solution.py
@@ -6,6 +6,17 @@
 
 screen_width = 0.5
 highest = lax.Precision.HIGHEST
+
+
+def in_blocks(array, dim, size):
+    before, after = (array.shape[:dim], array.shape[dim + 1 :])
+    return jnp.moveaxis(array.reshape(*before, size, -1, *after), dim, 0)
+
+
+def in_order(blocks, dim):
+    blocks = jnp.moveaxis(blocks, 0, dim)
+    lengths = blocks.shape
+    return blocks.reshape(*lengths[:dim], lengths[dim] * lengths[dim + 1], *lengths[dim + 2 :])
 
 
 def shifted(value, axis, steps):
@@ -57,7 +68,14 @@
     )
     real_part, imag_part = rotate(real_part, imag_part, cos_y, sin_y, "pzyx,yk->pzkx", True)
     part_re = lax.all_to_all(real_part, "slab", split_axis=2, concat_axis=1, tiled=True)
-    part_im = lax.all_to_all(imag_part, "slab", split_axis=2, concat_axis=1, tiled=True)
+    count_2, index = (lax.axis_size("slab"), lax.axis_index("slab"))
+    tiles = in_blocks(imag_part, 2, count_2)
+    outs = [tiles[index]]
+    for turn in range(1, count_2):
+        sent = tiles[(index + turn) % count_2]
+        outs.append(lax.ppermute(sent, "slab", [(i, (i + turn) % count_2) for i in range(count_2)]))
+    tiles = jnp.stack(outs)[(index - jnp.arange(count_2)) % count_2]
+    part_im = in_order(tiles, 1)
     band_rows = part_re.shape[2]
     row_index = lax.axis_index("slab") * band_rows + jnp.arange(band_rows, dtype=jnp.int32)
     freq_z = frequency(jnp.arange(depth, dtype=jnp.int32), depth)

time: 554 us -> 560 us (1.011)
  waiting for transfers between devices: 338 us -> 282 us
  starting transfers between devices: 38.6 us -> 87.3 us
  local copies, waits for them, and re-layouts: 37.2 us -> 50.5 us
    ppermute x0 -> x14, waiting for transfers between devices: none -> 113 us  [potentials(): lax.ppermute(sent, 'slab', [(i, (i + turn) % count_2) for i in range(coun...]
    all_to_all x2, waiting for transfers between devices: 90.9 us -> 0.01 us  [potentials(): lax.all_to_all(real_part, 'slab', split_axis=2, concat_axis=1, tiled=True)]
    all_to_all x2 -> x0, waiting for transfers between devices: 79.2 us -> none  [potentials(): lax.all_to_all(imag_part, 'slab', split_axis=2, concat_axis=1, tiled=True)]
    ppermute x0 -> x14, starting transfers between devices: none -> 56.9 us  [potentials(): lax.ppermute(sent, 'slab', [(i, (i + turn) % count_2) for i in range(coun...]
    all_to_all x2 -> x0, starting transfers between devices: 11.7 us -> none  [potentials(): lax.all_to_all(imag_part, 'slab', split_axis=2, concat_axis=1, tiled=True)]
    unnamed x18 -> x36, local copies, waits for them, and re-layouts: 0.04 us -> 9.02 us
    gather x0 -> x2, local copies, waits for them, and re-layouts: none -> 5.71 us  [potentials(): tiles = jnp.stack(outs)[(index - jnp.arange(count_2)) % count_2]]
  transfers between devices with their start and end apart: 9 -> 21, of which waited for: 8 -> 10; matrix products, arithmetic and copies ran while one was open for 12% -> 13% of each run, Pallas kernels for 0% -> 0%
where the time goes in v1:
time: 560 us; the launch traced here: 551 us
  waiting for transfers between devices  282 us (50%)
  matrix products  118 us (21%)
  starting transfers between devices  87.3 us (16%)
  local copies, waits for them, and re-layouts  50.5 us (9%)
  other arithmetic  11.9 us (2%)
    ppermute x14, waiting for transfers between devices, potentials(): lax.ppermute(sent, 'slab', [(i, (i + turn) % count_2) for i in range(coun...  113 us
    all_to_all x2, waiting for transfers between devices, potentials(): lax.all_to_all(part_im, 'slab', split_axis=1, concat_axis=2, tiled=True)  90.1 us
    all_to_all x2, waiting for transfers between devices, potentials(): lax.all_to_all(part_re, 'slab', split_axis=1, concat_axis=2, tiled=True)  79.2 us
    ppermute x14, starting transfers between devices, potentials(): lax.ppermute(sent, 'slab', [(i, (i + turn) % count_2) for i in range(coun...  56.9 us
    dot_general x8, matrix products, rotate(): imag_sin = jnp.einsum(form, imag_part, sine_table, precision=highest)  25.1 us
    dot_general x8, matrix products, rotate(): imag_cos = jnp.einsum(form, imag_part, cosine, precision=highest)  21.9 us
    dot_general x8, matrix products, rotate(): real_sin = jnp.einsum(form, real_part, sine_table, precision=highest)  18.1 us
    dot_general x8, matrix products, rotate(): real_cos = jnp.einsum(form, real_part, cosine, precision=highest)  17.8 us
  transfers between devices with their start and end apart: 21, of which 10 were waited for; matrix products, arithmetic and copies ran while one was open for 13% of the time, Pallas kernels for 0%

profile of v1, /device:TPU:0, one launch (start us, length us, event | category | flops | bytes accessed | tf_op | source)
XLA Modules:
  0.0 550.7 jit_solution(18144979933912655045)
XLA Ops:
  18.6 7.3 %all-to-all-start = ((f32[2,16,128,128]{3,1,0,2:T(8,128)}), f32[2,16,128,128]{3,1,0,2:T(8,128)}, u32[]{:S(2)}, u32[]{:S(2)}) async-start(f32[2,16,128,128]{3,1,0,2:T(8,128)} %copy.130), calls=%async_computation | async-start | bytes 4194304 | tf_op jit(solution)/shard_map/all_to_all | solution.py:70
  31.6 4.7 collective-permute-start.6
  41.6 45.8 %collective-permute-done = f32[2,16,16,128]{3,2,1,0:T(8,128)} collective-permute-done((f32[2,16,16,128]{3,2,1,0:T(8,128)}, f32[2,16,16,128]{3,2,1,0:T(8,128)}, u32[]{:S(2)}, u32[]{:S(2)}) %collective-permute-start) | collective-permute-done | bytes 262176 | tf_op jit(solution)/shard_map/ppermute | solution.py:76
  87.5 9.3 %collective-permute-start.2 = (f32[2,16,16,128]{3,2,1,0:T(8,128)}, f32[2,16,16,128]{3,2,1,0:T(8,128)S(1)}, u32[]{:S(2)}, u32[]{:S(2)}) collective-permute-start(f32[2,16,16,128]{3,2,1,0:T(8,128)} %get-tuple-element.11), channel_id=1, source_target_pairs={{0,12},{4,16},{8,20},{12,24},{16,28},{20,0},{24,4},{28,8},{1,13},{... | collective-permute-start | bytes 786440 | tf_op jit(solution)/shard_map/ppermute | solution.py:76
  98.4 5.4 collective-permute-start.3
  105.4 9.9 %collective-permute-done.2 = f32[2,16,16,128]{3,2,1,0:T(8,128)S(1)} collective-permute-done((f32[2,16,16,128]{3,2,1,0:T(8,128)}, f32[2,16,16,128]{3,2,1,0:T(8,128)S(1)}, u32[]{:S(2)}, u32[]{:S(2)}) %collective-permute-start.2) | collective-permute-done | bytes 262176 | tf_op jit(solution)/shard_map/ppermute | solution.py:76
  116.1 3.0 collective-permute-done.3
  123.9 3.6 gather_fusion
  136.3 2.9 subtract_multiply_fusion.1
  139.2 5.2 add_multiply_fusion.1
  151.9 4.9 all-to-all-start.1
  156.8 3.7 fusion.26
  165.4 39.3 %all-to-all-done.1 = f32[2,128,16,128]{3,2,0,1:T(8,128)} async-done(((f32[2,128,16,128]{3,2,0,1:T(8,128)}), f32[2,128,16,128]{3,2,0,1:T(8,128)}, u32[]{:S(2)}, u32[]{:S(2)}) %all-to-all-start.1) | async-done | bytes 2097184 | tf_op jit(solution)/shard_map/all_to_all | solution.py:92
  204.8 4.4 all-to-all-start.2
  209.4 3.3 copy.144
  212.6 44.3 %all-to-all-done.2 = f32[2,128,16,128]{3,2,0,1:T(8,128)} async-done(((f32[2,128,16,128]{3,2,0,1:T(8,128)}), f32[2,128,16,128]{3,2,0,1:T(8,128)}, u32[]{:S(2)}, u32[]{:S(2)}) %all-to-all-start.2) | async-done | bytes 2097184 | tf_op jit(solution)/shard_map/all_to_all | solution.py:93
  277.0 4.3 fusion
  297.2 4.3 all-to-all-start.3
  309.6 3.3 collective-permute-start.14
  314.0 33.4 %collective-permute-done.8 = f32[2,16,16,128]{3,2,1,0:T(8,128)S(1)} collective-permute-done((f32[2,16,16,128]{3,2,1,0:T(8,128)S(1)}, f32[2,16,16,128]{3,2,1,0:T(8,128)S(1)}, u32[]{:S(2)}, u32[]{:S(2)}) %collective-permute-start.8) | collective-permute-done | bytes 262176 | tf_op jit(solution)/shard_map/ppermute | solution.py:76
  347.5 19.6 %collective-permute-start.10 = (f32[2,16,16,128]{3,2,1,0:T(8,128)S(1)}, f32[2,16,16,128]{3,2,1,0:T(8,128)S(1)}, u32[]{:S(2)}, u32[]{:S(2)}) collective-permute-start(f32[2,16,16,128]{3,2,1,0:T(8,128)S(1)} %get-tuple-element.18), channel_id=1, source_target_pairs={{0,12},{4,16},{8,20},{12,24},{16,28},{20,0},{24,4},{28,8},{1,13},{... | collective-permute-start | bytes 786440 | tf_op jit(solution)/shard_map/ppermute | solution.py:76
  367.1 6.0 %collective-permute-start.11 = (f32[2,16,16,128]{3,2,1,0:T(8,128)S(1)}, f32[2,16,16,128]{3,2,1,0:T(8,128)S(1)}, u32[]{:S(2)}, u32[]{:S(2)}) collective-permute-start(f32[2,16,16,128]{3,2,1,0:T(8,128)S(1)} %get-tuple-element.17), channel_id=1, source_target_pairs={{0,16},{4,20},{8,24},{12,28},{16,0},{20,4},{24,8},{28,12},{1,17},{... | collective-permute-start | bytes 786440 | tf_op jit(solution)/shard_map/ppermute | solution.py:76
  373.1 17.3 %collective-permute-done.10 = f32[2,16,16,128]{3,2,1,0:T(8,128)S(1)} collective-permute-done((f32[2,16,16,128]{3,2,1,0:T(8,128)S(1)}, f32[2,16,16,128]{3,2,1,0:T(8,128)S(1)}, u32[]{:S(2)}, u32[]{:S(2)}) %collective-permute-start.10) | collective-permute-done | bytes 262176 | tf_op jit(solution)/shard_map/ppermute | solution.py:76
  390.5 3.7 collective-permute-done.11
  405.2 2.9 subtract_multiply_fusion
  408.1 5.2 add_multiply_fusion
  420.9 4.8 all-to-all-start.4
  425.7 3.7 fusion.10
  434.4 39.9 %all-to-all-done.4 = f32[2,128,16,128]{3,2,0,1:T(8,128)} async-done(((f32[2,128,16,128]{3,2,0,1:T(8,128)}), f32[2,128,16,128]{3,2,0,1:T(8,128)}, u32[]{:S(2)}, u32[]{:S(2)}) %all-to-all-start.4) | async-done | bytes 2097184 | tf_op jit(solution)/shard_map/all_to_all | solution.py:92
  474.2 4.5 all-to-all-start.5
  480.6 45.8 %all-to-all-done.5 = f32[2,128,16,128]{3,2,0,1:T(8,128)} async-done(((f32[2,128,16,128]{3,2,0,1:T(8,128)}), f32[2,128,16,128]{3,2,0,1:T(8,128)}, u32[]{:S(2)}, u32[]{:S(2)}) %all-to-all-start.5) | async-done | bytes 2097184 | tf_op jit(solution)/shard_map/all_to_all | solution.py:93
  546.1 2.8 fusion.1
  (126 shorter events, 151.2 us)
Async XLA Ops:
  11.5 2.2 copy-start.1
  18.6 110.7 %all-to-all-start = ((f32[2,16,128,128]{3,1,0,2:T(8,128)}), f32[2,16,128,128]{3,1,0,2:T(8,128)}, u32[]{:S(2)}, u32[]{:S(2)}) async-start(f32[2,16,128,128]{3,1,0,2:T(8,128)} %copy.130), calls=%async_computation | async-start | bytes 4194304 | tf_op jit(solution)/shard_map/all_to_all | solution.py:70
  25.9 2.2 copy-start.2
  31.6 91.5 %collective-permute-start.6 = (f32[2,16,16,128]{3,2,1,0:T(8,128)}, f32[2,16,16,128]{3,2,1,0:T(8,128)S(1)}, u32[]{:S(2)}, u32[]{:S(2)}) collective-permute-start(f32[2,16,16,128]{3,2,1,0:T(8,128)} %get-tuple-element.7), channel_id=1, source_target_pairs={{0,28},{4,0},{8,4},{12,8},{16,12},{20,16},{24,20},{28,24},{1,29},{... | collective-permute-start | bytes 786440 | tf_op jit(solution)/shard_map/ppermute | solution.py:76
  36.3 85.1 %collective-permute-start.5 = (f32[2,16,16,128]{3,2,1,0:T(8,128)}, f32[2,16,16,128]{3,2,1,0:T(8,128)}, u32[]{:S(2)}, u32[]{:S(2)}) collective-permute-start(f32[2,16,16,128]{3,2,1,0:T(8,128)} %get-tuple-element.8), channel_id=1, source_target_pairs={{0,24},{4,28},{8,0},{12,4},{16,8},{20,12},{24,16},{28,20},{1,25},{... | collective-permute-start | bytes 786440 | tf_op jit(solution)/shard_map/ppermute | solution.py:76
  36.9 82.9 %collective-permute-start.4 = (f32[2,16,16,128]{3,2,1,0:T(8,128)}, f32[2,16,16,128]{3,2,1,0:T(8,128)}, u32[]{:S(2)}, u32[]{:S(2)}) collective-permute-start(f32[2,16,16,128]{3,2,1,0:T(8,128)} %get-tuple-element.9), channel_id=1, source_target_pairs={{0,20},{4,24},{8,28},{12,0},{16,4},{20,8},{24,12},{28,16},{1,21},{... | collective-permute-start | bytes 786440 | tf_op jit(solution)/shard_map/ppermute | solution.py:76
  36.9 61.5 %collective-permute-start.1 = (f32[2,16,16,128]{3,2,1,0:T(8,128)}, f32[2,16,16,128]{3,2,1,0:T(8,128)}, u32[]{:S(2)}, u32[]{:S(2)}) collective-permute-start(f32[2,16,16,128]{3,2,1,0:T(8,128)} %get-tuple-element.12), channel_id=1, source_target_pairs={{0,8},{4,12},{8,16},{12,20},{16,24},{20,28},{24,0},{28,4},{1,9},{5... | collective-permute-start | bytes 786440 | tf_op jit(solution)/shard_map/ppermute | solution.py:76
  38.4 49.1 %collective-permute-start = (f32[2,16,16,128]{3,2,1,0:T(8,128)}, f32[2,16,16,128]{3,2,1,0:T(8,128)}, u32[]{:S(2)}, u32[]{:S(2)}) collective-permute-start(f32[2,16,16,128]{3,2,1,0:T(8,128)} %get-tuple-element.13), channel_id=1, source_target_pairs={{0,4},{4,8},{8,12},{12,16},{16,20},{20,24},{24,28},{28,0},{1,5},{5... | collective-permute-start | bytes 786440 | tf_op jit(solution)/shard_map/ppermute | solution.py:76
  87.5 27.9 %collective-permute-start.2 = (f32[2,16,16,128]{3,2,1,0:T(8,128)}, f32[2,16,16,128]{3,2,1,0:T(8,128)S(1)}, u32[]{:S(2)}, u32[]{:S(2)}) collective-permute-start(f32[2,16,16,128]{3,2,1,0:T(8,128)} %get-tuple-element.11), channel_id=1, source_target_pairs={{0,12},{4,16},{8,20},{12,24},{16,28},{20,0},{24,4},{28,8},{1,13},{... | collective-permute-start | bytes 786440 | tf_op jit(solution)/shard_map/ppermute | solution.py:76
  98.4 20.6 %collective-permute-start.3 = (f32[2,16,16,128]{3,2,1,0:T(8,128)}, f32[2,16,16,128]{3,2,1,0:T(8,128)S(1)}, u32[]{:S(2)}, u32[]{:S(2)}) collective-permute-start(f32[2,16,16,128]{3,2,1,0:T(8,128)} %get-tuple-element.10), channel_id=1, source_target_pairs={{0,16},{4,20},{8,24},{12,28},{16,0},{20,4},{24,8},{28,12},{1,17},{... | collective-permute-start | bytes 786440 | tf_op jit(solution)/shard_map/ppermute | solution.py:76
  129.3 7.0 %copy-start.6 = (f32[2,8,16,16,128]{4,3,2,1,0:T(8,128)}, f32[2,8,16,16,128]{4,3,2,1,0:T(8,128)S(1)}, u32[]{:S(2)}) copy-start(f32[2,8,16,16,128]{4,3,2,1,0:T(8,128)S(1)} %copy.135) | copy-start | bytes 6291460
  139.2 5.2 copy-start.8
  151.9 52.8 %all-to-all-start.1 = ((f32[2,128,16,128]{3,2,0,1:T(8,128)}), f32[2,128,16,128]{3,2,0,1:T(8,128)}, u32[]{:S(2)}, u32[]{:S(2)}) async-start(f32[2,128,16,128]{3,2,0,1:T(8,128)} %copy.143), calls=%async_computation.1 | async-start | bytes 4194304 | tf_op jit(solution)/shard_map/all_to_all | solution.py:92
  165.4 43.7 %copy-start = (f32[2,16,128,128]{3,2,1,0:T(8,128)S(1)}, f32[2,16,128,128]{3,2,1,0:T(8,128)}, u32[]{:S(2)}) copy-start(f32[2,16,128,128]{3,2,1,0:T(8,128)} %param.1) | copy-start | bytes 6291460
  204.8 52.2 %all-to-all-start.2 = ((f32[2,128,16,128]{3,2,0,1:T(8,128)}), f32[2,128,16,128]{3,2,0,1:T(8,128)}, u32[]{:S(2)}, u32[]{:S(2)}) async-start(f32[2,128,16,128]{3,2,0,1:T(8,128)} %copy.148), calls=%async_computation.2 | async-start | bytes 4194304 | tf_op jit(solution)/shard_map/all_to_all | solution.py:93
  209.1 67.8 %collective-permute-start.7 = (f32[2,16,128,128]{3,2,1,0:T(8,128)S(1)}, f32[2,16,128,128]{3,2,1,0:T(8,128)}, u32[]{:S(2)}, u32[]{:S(2)}) collective-permute-start(f32[2,16,128,128]{3,2,1,0:T(8,128)S(1)} %copy-done), channel_id=1, source_target_pairs={{0,1},{1,2},{2,3},{3,0},{4,5},{5,6},{6,7},{7,4},{8,9},{9,10},{10,1... | collective-permute-start | bytes 6291464 | tf_op jit(solution)/shard_map/ppermute | solution.py:25
  258.8 2.2 copy-start.9
  290.2 2.2 copy-start.3
  297.2 101.0 %all-to-all-start.3 = ((f32[2,16,128,128]{3,1,0,2:T(8,128)}), f32[2,16,128,128]{3,1,0,2:T(8,128)}, u32[]{:S(2)}, u32[]{:S(2)}) async-start(f32[2,16,128,128]{3,1,0,2:T(8,128)} %copy.156), calls=%async_computation.3 | async-start | bytes 4194304 | tf_op jit(solution)/shard_map/all_to_all | solution.py:70
  301.5 2.2 copy-start.4
  306.2 41.3 %collective-permute-start.8 = (f32[2,16,16,128]{3,2,1,0:T(8,128)S(1)}, f32[2,16,16,128]{3,2,1,0:T(8,128)S(1)}, u32[]{:S(2)}, u32[]{:S(2)}) collective-permute-start(f32[2,16,16,128]{3,2,1,0:T(8,128)S(1)} %get-tuple-element.20), channel_id=1, source_target_pairs={{0,4},{4,8},{8,12},{12,16},{16,20},{20,24},{24,28},{28,0},{1,5},{5... | collective-permute-start | bytes 786440 | tf_op jit(solution)/shard_map/ppermute | solution.py:76
  308.1 59.0 %collective-permute-start.9 = (f32[2,16,16,128]{3,2,1,0:T(8,128)S(1)}, f32[2,16,16,128]{3,2,1,0:T(8,128)S(1)}, u32[]{:S(2)}, u32[]{:S(2)}) collective-permute-start(f32[2,16,16,128]{3,2,1,0:T(8,128)S(1)} %get-tuple-element.19), channel_id=1, source_target_pairs={{0,8},{4,12},{8,16},{12,20},{16,24},{20,28},{24,0},{28,4},{1,9},{5... | collective-permute-start | bytes 786440 | tf_op jit(solution)/shard_map/ppermute | solution.py:76
  309.6 84.7 %collective-permute-start.14 = (f32[2,16,16,128]{3,2,1,0:T(8,128)S(1)}, f32[2,16,16,128]{3,2,1,0:T(8,128)S(1)}, u32[]{:S(2)}, u32[]{:S(2)}) collective-permute-start(f32[2,16,16,128]{3,2,1,0:T(8,128)S(1)} %get-tuple-element.14), channel_id=1, source_target_pairs={{0,28},{4,0},{8,4},{12,8},{16,12},{20,16},{24,20},{28,24},{1,29},{... | collective-permute-start | bytes 786440 | tf_op jit(solution)/shard_map/ppermute | solution.py:76
  312.9 81.3 %collective-permute-start.13 = (f32[2,16,16,128]{3,2,1,0:T(8,128)S(1)}, f32[2,16,16,128]{3,2,1,0:T(8,128)S(1)}, u32[]{:S(2)}, u32[]{:S(2)}) collective-permute-start(f32[2,16,16,128]{3,2,1,0:T(8,128)S(1)} %get-tuple-element.15), channel_id=1, source_target_pairs={{0,24},{4,28},{8,0},{12,4},{16,8},{20,12},{24,16},{28,20},{1,25},{... | collective-permute-start | bytes 786440 | tf_op jit(solution)/shard_map/ppermute | solution.py:76
  313.0 81.2 %collective-permute-start.12 = (f32[2,16,16,128]{3,2,1,0:T(8,128)S(1)}, f32[2,16,16,128]{3,2,1,0:T(8,128)S(1)}, u32[]{:S(2)}, u32[]{:S(2)}) collective-permute-start(f32[2,16,16,128]{3,2,1,0:T(8,128)S(1)} %get-tuple-element.16), channel_id=1, source_target_pairs={{0,20},{4,24},{8,28},{12,0},{16,4},{20,8},{24,12},{28,16},{1,21},{... | collective-permute-start | bytes 786440 | tf_op jit(solution)/shard_map/ppermute | solution.py:76
  347.5 43.0 %collective-permute-start.10 = (f32[2,16,16,128]{3,2,1,0:T(8,128)S(1)}, f32[2,16,16,128]{3,2,1,0:T(8,128)S(1)}, u32[]{:S(2)}, u32[]{:S(2)}) collective-permute-start(f32[2,16,16,128]{3,2,1,0:T(8,128)S(1)} %get-tuple-element.18), channel_id=1, source_target_pairs={{0,12},{4,16},{8,20},{12,24},{16,28},{20,0},{24,4},{28,8},{1,13},{... | collective-permute-start | bytes 786440 | tf_op jit(solution)/shard_map/ppermute | solution.py:76
  367.1 27.0 %collective-permute-start.11 = (f32[2,16,16,128]{3,2,1,0:T(8,128)S(1)}, f32[2,16,16,128]{3,2,1,0:T(8,128)S(1)}, u32[]{:S(2)}, u32[]{:S(2)}) collective-permute-start(f32[2,16,16,128]{3,2,1,0:T(8,128)S(1)} %get-tuple-element.17), channel_id=1, source_target_pairs={{0,16},{4,20},{8,24},{12,28},{16,0},{20,4},{24,8},{28,12},{1,17},{... | collective-permute-start | bytes 786440 | tf_op jit(solution)/shard_map/ppermute | solution.py:76
  398.2 7.0 %copy-start.5 = (f32[2,8,16,16,128]{4,3,2,1,0:T(8,128)}, f32[2,8,16,16,128]{4,3,2,1,0:T(8,128)S(1)}, u32[]{:S(2)}) copy-start(f32[2,8,16,16,128]{4,3,2,1,0:T(8,128)S(1)} %copy.161) | copy-start | bytes 6291460
  408.1 5.2 copy-start.7
  420.9 53.4 %all-to-all-start.4 = ((f32[2,128,16,128]{3,2,0,1:T(8,128)}), f32[2,128,16,128]{3,2,0,1:T(8,128)}, u32[]{:S(2)}, u32[]{:S(2)}) async-start(f32[2,128,16,128]{3,2,0,1:T(8,128)} %copy.169), calls=%async_computation.4 | async-start | bytes 4194304 | tf_op jit(solution)/shard_map/all_to_all | solution.py:92
  474.2 52.2 %all-to-all-start.5 = ((f32[2,128,16,128]{3,2,0,1:T(8,128)}), f32[2,128,16,128]{3,2,0,1:T(8,128)}, u32[]{:S(2)}, u32[]{:S(2)}) async-start(f32[2,128,16,128]{3,2,0,1:T(8,128)} %copy.174), calls=%async_computation.5 | async-start | bytes 4194304 | tf_op jit(solution)/shard_map/all_to_all | solution.py:93
  546.0 2.8 copy-start.10
